TPU v7x, 128 devices: a whole 4x4x4 slice. The times are simulated.
128 devices in a mesh: slab: 16 (over z_lo, x, core), buddy: 8 (over y, z_hi).
Axes of the slice: x: 4, y: 4, z: 4 (z_hi: 2, z_lo: 2; z = z_hi * 2 + z_lo), core: 2. Of those that a mesh axis runs over, the one named last changes fastest.
Arguments:
- checkpoint: float32 [64, 5, 128, 4, 256], P('buddy', None, 'slab'), may hold values from -6 to 6
- slot_block: int32 [8, 8], replicated, may hold values from 0 to 63, as said below
- live_state: float32 [8, 5, 128, 32, 256], P('buddy', None, 'slab'), may hold values from -6 to 6
- levels: int32 [2, 8, 3], P(None, 'buddy'), may hold values from 0 to 2
- coefficients: float32 [2, 8], P(None, 'buddy'), may hold values from 0.3 to 1
- tile_owner: int32 [16, 16], P('slab'), may hold values from 0 to 7, as said below
Outputs:
- recovered: float32 [8, 5, 128, 32, 256], P('buddy', None, 'slab')
- combined: float32 [32, 5, 128, 2, 256], P('buddy', None, 'slab')
Inputs may be any that keep to these rules, and one draw needn't show every extreme that they name: `slot_block`: row h lists the blocks in the 8 slots of holder h, block j of grid g written g * 8 + j. Every block is held exactly once, never by its own grid's holder; one holder keeps at most 3 blocks of one grid, and some holder keeps exactly 3 of some grid. `tile_owner`: no reader reads more than 4 tiles of one slab, and in every slab some reader reads exactly 4.
All inputs are finite; a program needn't handle non-finite values.
Results may differ from a plain program's by a relative error of at most 0.000096.
Values sent between devices are 32-bit elements; how exact they have to be, the bound alone decides.
A program may use at most 192 MiB of HBM per device.

v0:
```python
import functools

import jax
import jax.numpy as jnp
from jax import lax
from jax.experimental import pallas as pl
from jax.experimental.pallas import tpu as pltpu
from jax.sharding import PartitionSpec as P

MESH = pl.DeviceIdType.MESH
VELOCITY = (0.3, -0.2, 0.45)
FIELDS = 5
CZ = 8
CY = 32
CX = 256
HALO = 4
PEERS = 7
OFFSETS = ((2, 1), (2, 0), (1, 1), (3, 1), (0, 1), (1, 0), (3, 0))


def stencil(levels_ref, kind):
    inverse = []
    for axis in range(3):
        level = levels_ref[kind, 0, axis]
        inverse.append(jnp.where(level == 0, 1.0, jnp.where(level == 1, 2.0, 4.0)).astype(jnp.float32))
    denominator = (abs(VELOCITY[0]) + 1.0) * inverse[0] + (abs(VELOCITY[1]) + 1.0) * inverse[1]
    denominator = denominator + (abs(VELOCITY[2]) + 1.0) * inverse[2]
    step = jnp.max(1.0 / jnp.full((8, 128), denominator, jnp.float32))
    middle = -step * denominator
    sides = []
    for axis in range(3):
        scaled = step * inverse[axis]
        half = 0.5 * (abs(VELOCITY[axis]) + 1.0)
        sides.append(
            (
                scaled * (half - 0.5 * VELOCITY[axis]),
                scaled * (half + 0.5 * VELOCITY[axis]),
                scaled * -0.5,
            )
        )
    return middle, sides


def section(source, base, scalars, share, first, last, write):
    middle, sides = scalars
    middle = middle * share
    sides = [tuple(value * share for value in side) for side in sides]

    def one_layer(z, carry):
        def own_terms(field):
            q = source[field, z]
            out = base[field, z] + middle * q
            shifted = (
                (pltpu.roll(q, CX - 1, 1), pltpu.roll(q, 1, 1)),
                (pltpu.roll(q, CY - 1, 0), pltpu.roll(q, 1, 0)),
                (source[field, z + 1], source[field, z - 1]),
            )
            for (plus, minus), side in zip(shifted, sides):
                out = out + (side[0] * plus + side[1] * minus)
            return out, shifted

        pressure, around = own_terms(4)
        pushes = [side[2] * (plus - minus) for (plus, minus), side in zip(around, sides)]
        spread = None
        results = [None] * FIELDS
        for axis in range(3):
            out, around = own_terms(1 + axis)
            results[1 + axis] = out + pushes[axis]
            part = sides[axis][2] * (around[axis][0] - around[axis][1])
            spread = part if spread is None else spread + part
        results[4] = pressure + spread
        results[0] = own_terms(0)[0] + spread
        write(z, results)
        return carry

    lax.fori_loop(first, last, one_layer, 0)


def kernel(
    inverse_ref,
    tiles_ref,
    levels_ref,
    coefficients_ref,
    checkpoint_ref,
    live_ref,
    recovered_ref,
    combined_ref,
    lines_0,
    lines_1,
    lines_2,
    lines_3,
    lines_4,
    packed,
    lost,
    live,
    stage_a,
    stage_b,
    advanced,
    recovered,
    weighted,
    arrived,
    total,
    chosen,
    local_sem,
    send1,
    recv1,
    send2,
    recv2,
    send3,
    recv3,
    send4,
    recv4,
    halo_send,
    halo_recv,
    live_send,
    live_recv,
):
    lines = (lines_0, lines_1, lines_2, lines_3, lines_4)
    slab = lax.axis_index("slab")
    me = lax.axis_index("buddy")
    slabs = lax.axis_size("slab")
    row, half = me // 2, me % 2
    above = (slab + 1) % slabs
    below = (slab + slabs - 1) % slabs

    def at(offset):
        return ((row + offset[0]) % 4) * 2 + (half + offset[1]) % 2

    peers = [at(offset) for offset in OFFSETS]
    sources = [at(((4 - offset[0]) % 4, offset[1])) for offset in OFFSETS]

    live_in = pltpu.make_async_copy(live_ref.at[0], live.at[:, pl.ds(HALO, CZ)], local_sem.at[0])
    live_in.start()
    own_copies = []
    for field in range(FIELDS):
        copy = pltpu.make_async_copy(
            checkpoint_ref.at[:, field, me], lines[field].at[pl.ds(me * 8, 8)], local_sem.at[1 + field]
        )
        copy.start()
        own_copies.append(copy)

    barrier = pltpu.get_barrier_semaphore()
    for peer in peers:
        pl.semaphore_signal(barrier, inc=1, device_id={"buddy": peer}, device_id_type=MESH)
    for neighbour in (below, above):
        pl.semaphore_signal(barrier, inc=1, device_id={"slab": neighbour}, device_id_type=MESH)
    pl.semaphore_wait(barrier, PEERS + 2)

    first_copies = []
    for field in range(FIELDS):
        for i, peer in enumerate(peers):
            copy = pltpu.make_async_remote_copy(
                src_ref=checkpoint_ref.at[:, field, peer],
                dst_ref=lines[field].at[pl.ds(me * 8, 8)],
                send_sem=send1.at[field, i],
                recv_sem=recv1.at[field, i],
                device_id={"buddy": peer},
                device_id_type=MESH,
            )
            copy.start()
            first_copies.append(copy)
    live_copies = []
    for way, (neighbour, start, to) in enumerate(((below, 0, HALO + CZ), (above, CZ - HALO, 0))):
        copy = pltpu.make_async_remote_copy(
            src_ref=live_ref.at[0, :, pl.ds(start, HALO)],
            dst_ref=live.at[:, pl.ds(to, HALO)],
            send_sem=live_send.at[way],
            recv_sem=live_recv.at[way],
            device_id={"slab": neighbour},
            device_id_type=MESH,
        )
        copy.start()
        live_copies.append(copy)

    second_copies = []
    for field in range(FIELDS):
        own_copies[field].wait()
        for i in range(PEERS):
            first_copies[field * PEERS + i].wait_recv()
        for i, peer in enumerate(peers):
            for block in range(8):
                packed[field, i, pl.ds(block * 4, 4), :] = lines[field][inverse_ref[peer * 8 + block]]
            copy = pltpu.make_async_remote_copy(
                src_ref=packed.at[field, i],
                dst_ref=lost.at[field, HALO + me],
                send_sem=send2.at[field, i],
                recv_sem=recv2.at[field, i],
                device_id={"buddy": peer},
                device_id_type=MESH,
            )
            copy.start()
            second_copies.append(copy)
        for block in range(8):
            lost[field, HALO + me, pl.ds(block * 4, 4), :] = lines[field][inverse_ref[me * 8 + block]]

    def to_buffer(buffer):
        def write(z, results):
            for field in range(FIELDS):
                buffer[field, z] = results[field]

        return write

    def to_advanced(z, results):
        for field in range(FIELDS):
            advanced[z - HALO, field] = results[field]

    share = coefficients_ref[0, 0]
    live_share = coefficients_ref[1, 0]

    def to_recovered(z, results):
        for field in range(FIELDS):
            recovered[field, z - HALO] = results[field]
            weighted[z - HALO, field] = share * results[field] + live_share * advanced[z - HALO, field]

    def run_sections(state, scalars, finish, between):
        section(state, state, scalars, 0.25, 1, 2 * HALO + CZ - 1, to_buffer(stage_a))
        between(0)
        section(stage_a, state, scalars, 1.0 / 3.0, 2, 2 * HALO + CZ - 2, to_buffer(stage_b))
        between(1)
        section(stage_b, state, scalars, 0.5, 3, 2 * HALO + CZ - 3, to_buffer(stage_a))
        between(2)
        section(stage_a, state, scalars, 1.0, HALO, HALO + CZ, finish)
        between(3)

    halo_copies = []

    def pass_halos(field):
        for i in range(PEERS):
            second_copies[field * PEERS + i].wait_recv()
        for way, (neighbour, start, to) in enumerate(((below, HALO, HALO + CZ), (above, CZ, 0))):
            copy = pltpu.make_async_remote_copy(
                src_ref=lost.at[field, pl.ds(start, HALO)],
                dst_ref=lost.at[field, pl.ds(to, HALO)],
                send_sem=halo_send.at[field, way],
                recv_sem=halo_recv.at[field, way],
                device_id={"slab": neighbour},
                device_id_type=MESH,
            )
            copy.start()
            halo_copies.append(copy)

    live_in.wait()
    for copy in live_copies:
        copy.wait_recv()
    run_sections(live, stencil(levels_ref, 1), to_advanced, pass_halos)
    pass_halos(4)
    lost_scalars = stencil(levels_ref, 0)
    for copy in halo_copies:
        copy.wait_recv()
    run_sections(lost, lost_scalars, to_recovered, lambda step: None)

    recovered_out = pltpu.make_async_copy(recovered, recovered_ref, local_sem.at[0])
    recovered_out.start()

    third_copies = []
    for field in range(FIELDS):
        for i, peer in enumerate(peers):
            copy = pltpu.make_async_remote_copy(
                src_ref=weighted.at[peer, field],
                dst_ref=arrived.at[field, i],
                send_sem=send3.at[field, i],
                recv_sem=recv3.at[field, i],
                device_id={"buddy": peer},
                device_id_type=MESH,
            )
            copy.start()
            third_copies.append(copy)

    for field in range(FIELDS):
        total[field, 16] = jnp.zeros((2, CX), jnp.float32)
    fourth_copies = []
    for field in range(FIELDS):
        summed = weighted[me, field]
        for i in range(PEERS):
            third_copies[field * PEERS + i].wait_recv()
            summed = summed + arrived[field, i]
        for tile in range(16):
            total[field, tile] = summed[2 * tile : 2 * tile + 2]
        for i, peer in enumerate(peers):
            for rank in range(4):
                chosen[field, i, pl.ds(rank * 2, 2), :] = total[field, tiles_ref[peer * 4 + rank]]
            copy = pltpu.make_async_remote_copy(
                src_ref=chosen.at[field, i],
                dst_ref=combined_ref.at[field, me],
                send_sem=send4.at[field, i],
                recv_sem=recv4.at[field, i],
                device_id={"buddy": peer},
                device_id_type=MESH,
            )
            copy.start()
            fourth_copies.append(copy)
        for rank in range(4):
            combined_ref[field, me, pl.ds(rank * 2, 2), :] = total[field, tiles_ref[me * 4 + rank]]

    for copy in fourth_copies:
        copy.wait()
    for copy in first_copies + second_copies + third_copies + live_copies + halo_copies:
        copy.wait_send()
    recovered_out.wait()


def body(checkpoint, slot_block, live_state, levels, coefficients, tile_owner):
    ids = jnp.arange(64, dtype=jnp.int32)
    inverse = jnp.sum(jnp.where(slot_block.reshape(1, 64) == ids[:, None], ids[None, :], 0), axis=1)
    owners = tile_owner[0]
    order = jnp.arange(16, dtype=jnp.int32)
    ranks = jnp.sum(
        jnp.where((owners[None, :] == owners[:, None]) & (order[None, :] < order[:, None]), 1, 0), axis=1
    )
    slots = owners * 4 + ranks
    seats = jnp.arange(32, dtype=jnp.int32)
    tiles = 16 + jnp.sum(jnp.where(slots[None, :] == seats[:, None], order[None, :] - 16, 0), axis=1)
    smem = pl.BlockSpec(memory_space=pltpu.SMEM)
    away = pl.BlockSpec(memory_space=pl.ANY)
    dma = pltpu.SemaphoreType.DMA
    recovered, combined = pl.pallas_call(
        kernel,
        name="recover_and_combine",
        out_shape=(
            jax.ShapeDtypeStruct((FIELDS, CZ, CY, CX), jnp.float32),
            jax.ShapeDtypeStruct((FIELDS, CZ, 8, CX), jnp.float32),
        ),
        in_specs=[smem, smem, smem, smem, away, away],
        out_specs=(away, pl.BlockSpec(memory_space=pltpu.VMEM)),
        scratch_shapes=[
            *[pltpu.VMEM((64, 4, CX), jnp.float32) for _ in range(FIELDS)],
            pltpu.VMEM((FIELDS, PEERS, CY, CX), jnp.float32),
            pltpu.VMEM((FIELDS, CZ + 2 * HALO, CY, CX), jnp.float32),
            pltpu.VMEM((FIELDS, CZ + 2 * HALO, CY, CX), jnp.float32),
            pltpu.VMEM((FIELDS, CZ + 2 * HALO, CY, CX), jnp.float32),
            pltpu.VMEM((FIELDS, CZ + 2 * HALO, CY, CX), jnp.float32),
            pltpu.VMEM((CZ, FIELDS, CY, CX), jnp.float32),
            pltpu.VMEM((FIELDS, CZ, CY, CX), jnp.float32),
            pltpu.VMEM((CZ, FIELDS, CY, CX), jnp.float32),
            pltpu.VMEM((FIELDS, PEERS, CY, CX), jnp.float32),
            pltpu.VMEM((FIELDS, 17, 2, CX), jnp.float32),
            pltpu.VMEM((FIELDS, PEERS, 8, CX), jnp.float32),
            dma((1 + FIELDS,)),
            dma((FIELDS, PEERS)),
            dma((FIELDS, PEERS)),
            dma((FIELDS, PEERS)),
            dma((FIELDS, PEERS)),
            dma((FIELDS, PEERS)),
            dma((FIELDS, PEERS)),
            dma((FIELDS, PEERS)),
            dma((FIELDS, PEERS)),
            dma((FIELDS, 2)),
            dma((FIELDS, 2)),
            dma((2,)),
            dma((2,)),
        ],
        compiler_params=pltpu.CompilerParams(
            collective_id=0, has_side_effects=True, vmem_limit_bytes=48 << 20
        ),
    )(inverse, tiles, levels, coefficients, checkpoint, live_state)
    combined = combined.reshape(FIELDS, CZ, 4, 2, CX).transpose(2, 0, 1, 3, 4)
    return recovered[None], combined


def solution(mesh):
    return jax.shard_map(
        body,
        mesh=mesh,
        in_specs=(
            P("buddy", None, "slab", None, None),
            P(),
            P("buddy", None, "slab", None, None),
            P(None, "buddy", None),
            P(None, "buddy"),
            P("slab", None),
        ),
        out_specs=(P("buddy", None, "slab", None, None), P("buddy", None, "slab", None, None)),
        check_vma=False,
    )
```

profile of v0, /device:TPU:7, one launch (start us, length us, event | category | flops | bytes accessed | tf_op | source)
XLA Modules:
  0.0 96.6 jit_solution(2996679225257050332)
XLA Ops:
  0.6 0.8 eq.45
  1.4 0.1 select_reduce_fusion.inverse_ref
  1.5 0.9 select_reduce_fusion.2
  2.4 0.7 fusion.1
  3.1 0.1 select_reduce_fusion.1
  3.2 0.7 copy.10.coefficients_ref
  3.9 0.0 copy-start
  3.9 1.3 %copy-done = f32[8,5,8,4,256]{4,3,2,1,0:T(4,128)S(1)} copy-done((f32[8,5,8,4,256]{4,3,2,1,0:T(4,128)S(1)}, f32[8,5,8,4,256]{4,3,2,1,0:T(4,128)}, u32[]{:S(2)}) %copy-start) | copy-done | bytes 1310744
  5.3 0.0 copy-start.1
  5.3 1.3 %copy-done.1 = f32[1,5,8,32,256]{4,3,2,1,0:T(8,128)S(1)} copy-done((f32[1,5,8,32,256]{4,3,2,1,0:T(8,128)S(1)}, f32[1,5,8,32,256]{4,3,2,1,0:T(8,128)}, u32[]{:S(2)}) %copy-start.1) | copy-done | bytes 1310744
  6.6 0.0 copy-start.2
  6.6 0.7 copy-done.2
  7.2 87.2 %recover_and_combine.1 = (f32[5,8,32,256]{3,2,1,0:T(8,128)S(1)}, f32[5,8,8,256]{3,2,1,0:T(8,128)S(1)}) custom-call(s32[64]{0:T(128)S(1)} %select_reduce_fusion.inverse_ref, s32[32]{0:T(128)S(1)} %broadcast_add_fusion.tiles_ref, s32[2,1,3]{2,1,0:T(1,128)S(1)} %copy-done.2, f32[2,1]{1,0:T(2,128)S(1)} %copy.10.coefficients_ref, ...), custom_call_target="tpu_custom_call" | custom-call | tf_op jit(solution)/shard_map/recover_and_combine/pallas_call | solution.py:316
  94.5 0.2 reshape.16
  94.7 0.9 copy.13
  95.6 1.1 %copy.15 = f32[1,5,8,32,256]{4,3,2,1,0:T(8,128)} copy(f32[1,5,8,32,256]{4,3,2,1,0:T(8,128)S(1)} %bitcast.13) | data formatting | bytes 2621440
  (2 shorter events, 0.0 us)
Async XLA Ops:
  3.9 1.3 %copy-start = (f32[8,5,8,4,256]{4,3,2,1,0:T(4,128)S(1)}, f32[8,5,8,4,256]{4,3,2,1,0:T(4,128)}, u32[]{:S(2)}) copy-start(f32[8,5,8,4,256]{4,3,2,1,0:T(4,128)} %checkpoint_ref.1) | copy-start | bytes 3932164
  5.3 1.3 %copy-start.1 = (f32[1,5,8,32,256]{4,3,2,1,0:T(8,128)S(1)}, f32[1,5,8,32,256]{4,3,2,1,0:T(8,128)}, u32[]{:S(2)}) copy-start(f32[1,5,8,32,256]{4,3,2,1,0:T(8,128)} %live_ref.1) | copy-start | bytes 3932164
  6.6 0.7 copy-start.2
where the time goes:
time: 98.2 us; the launch traced here: 96.6 us
  Pallas kernels  87.2 us (89%)
  local copies, waits for them, and re-layouts  6.96 us (7%)
  other arithmetic  1.79 us (2%)
    pallas_call x1, Pallas kernels, body(): pl.pallas_call(kernel, name='recover_and_combine', out_shape=(jax.ShapeDt...  87.2 us
    unnamed x8, local copies, waits for them, and re-layouts  5.11 us

commit v1 on v0

--- a/solution.py
+++ b/solution.py
@@ -15,6 +15,8 @@
 CX = 256
 HALO = 4
 PEERS = 7
+ALONG = (0, 1, 2)
+ACROSS = (3, 4)
 OFFSETS = ((2, 1), (2, 0), (1, 1), (3, 1), (0, 1), (1, 0), (3, 0))
 
 
@@ -77,8 +79,8 @@
 
 
 def kernel(
-    inverse_ref,
-    tiles_ref,
+    slots_ref,
+    owners_ref,
     levels_ref,
     coefficients_ref,
     checkpoint_ref,
@@ -98,9 +100,16 @@
     advanced,
     recovered,
     weighted,
-    arrived,
+    far_in,
+    near_out,
+    near_in,
+    across_out,
+    across_in,
+    columns,
     total,
     chosen,
+    tables,
+    numbers,
     local_sem,
     send1,
     recv1,
@@ -110,6 +119,8 @@
     recv3,
     send4,
     recv4,
+    wrap_send,
+    wrap_recv,
     halo_send,
     halo_recv,
     live_send,
@@ -129,6 +140,22 @@
     peers = [at(offset) for offset in OFFSETS]
     sources = [at(((4 - offset[0]) % 4, offset[1])) for offset in OFFSETS]
 
+    wraps = ((slab % 8 == 0, below, 0, HALO + CZ), (slab % 8 == 7, above, HALO, -HALO))
+
+    barrier = pltpu.get_barrier_semaphore()
+    for peer in peers:
+        pl.semaphore_signal(barrier, inc=1, device_id={"buddy": peer}, device_id_type=MESH)
+    for neighbour in (below, above):
+        pl.semaphore_signal(barrier, inc=1, device_id={"slab": neighbour}, device_id_type=MESH)
+    for wrap, neighbour, _, _ in wraps:
+
+        @pl.when(wrap)
+        def _():
+            for peer in peers:
+                pl.semaphore_signal(
+                    barrier, inc=1, device_id={"slab": neighbour, "buddy": peer}, device_id_type=MESH
+                )
+
     live_in = pltpu.make_async_copy(live_ref.at[0], live.at[:, pl.ds(HALO, CZ)], local_sem.at[0])
     live_in.start()
     own_copies = []
@@ -139,12 +166,8 @@
         copy.start()
         own_copies.append(copy)
 
-    barrier = pltpu.get_barrier_semaphore()
-    for peer in peers:
-        pl.semaphore_signal(barrier, inc=1, device_id={"buddy": peer}, device_id_type=MESH)
-    for neighbour in (below, above):
-        pl.semaphore_signal(barrier, inc=1, device_id={"slab": neighbour}, device_id_type=MESH)
-    pl.semaphore_wait(barrier, PEERS + 2)
+    crossing = jnp.logical_or(wraps[0][0], wraps[1][0])
+    pl.semaphore_wait(barrier, jnp.where(crossing, 2 * PEERS + 2, PEERS + 2))
 
     first_copies = []
     for field in range(FIELDS):
@@ -172,14 +195,30 @@
         copy.start()
         live_copies.append(copy)
 
+    lanes = lax.broadcasted_iota(jnp.int32, (8, 128), 1)
+    held_in = jnp.zeros((8, 128), jnp.int32)
+    for slot in range(64):
+        held_in = jnp.where(lanes == slots_ref[slot // 8, slot % 8], slot, held_in)
+    tables[0:8] = held_in
+    owners = [owners_ref[0, tile] for tile in range(16)]
+    seated = jnp.full((8, 128), 16, jnp.int32)
+    for tile in range(16):
+        rank = sum([(owners[before] == owners[tile]).astype(jnp.int32) for before in range(tile)], 0)
+        seated = jnp.where(lanes == owners[tile] * 4 + rank, tile, seated)
+    tables[8:16] = seated
+    tables_in = pltpu.make_async_copy(tables, numbers, local_sem.at[1 + FIELDS])
+    tables_in.start()
+
+    tables_in.wait()
     second_copies = []
-    for field in range(FIELDS):
+
+    def pass_layers(field):
         own_copies[field].wait()
         for i in range(PEERS):
             first_copies[field * PEERS + i].wait_recv()
         for i, peer in enumerate(peers):
             for block in range(8):
-                packed[field, i, pl.ds(block * 4, 4), :] = lines[field][inverse_ref[peer * 8 + block]]
+                packed[field, i, pl.ds(block * 4, 4), :] = lines[field][numbers[0, peer * 8 + block]]
             copy = pltpu.make_async_remote_copy(
                 src_ref=packed.at[field, i],
                 dst_ref=lost.at[field, HALO + me],
@@ -191,7 +230,28 @@
             copy.start()
             second_copies.append(copy)
         for block in range(8):
-            lost[field, HALO + me, pl.ds(block * 4, 4), :] = lines[field][inverse_ref[me * 8 + block]]
+            packed[field, PEERS, pl.ds(block * 4, 4), :] = lines[field][numbers[0, me * 8 + block]]
+        lost[field, HALO + me] = packed[field, PEERS]
+        for i in range(PEERS + 1):
+            for way in range(2):
+                wrapped(field, i, way, "start")
+
+    def wrapped(field, i, way, action):
+        wrap, neighbour, first, to = wraps[way]
+        peer = me if i == PEERS else peers[i]
+        layer = me - first
+
+        @pl.when(jnp.logical_and(wrap, jnp.logical_and(layer >= 0, layer < HALO)))
+        def _():
+            copy = pltpu.make_async_remote_copy(
+                src_ref=packed.at[field, i],
+                dst_ref=lost.at[field, me + to],
+                send_sem=wrap_send.at[field, i],
+                recv_sem=wrap_recv.at[field, way, layer],
+                device_id={"slab": neighbour, "buddy": peer},
+                device_id_type=MESH,
+            )
+            copy.start() if action == "start" else copy.wait_send()
 
     def to_buffer(buffer):
         def write(z, results):
@@ -205,12 +265,12 @@
             advanced[z - HALO, field] = results[field]
 
     share = coefficients_ref[0, 0]
-    live_share = coefficients_ref[1, 0]
+    live_share = coefficients_ref[0, 1]
 
     def to_recovered(z, results):
         for field in range(FIELDS):
             recovered[field, z - HALO] = results[field]
-            weighted[z - HALO, field] = share * results[field] + live_share * advanced[z - HALO, field]
+            weighted[(z - HALO) // 2, (z - HALO) % 2, field] = share * results[field] + live_share * advanced[z - HALO, field]
 
     def run_sections(state, scalars, finish, between):
         section(state, state, scalars, 0.25, 1, 2 * HALO + CZ - 1, to_buffer(stage_a))
@@ -222,66 +282,184 @@
         section(stage_a, state, scalars, 1.0, HALO, HALO + CZ, finish)
         between(3)
 
-    halo_copies = []
-
     def pass_halos(field):
         for i in range(PEERS):
             second_copies[field * PEERS + i].wait_recv()
-        for way, (neighbour, start, to) in enumerate(((below, HALO, HALO + CZ), (above, CZ, 0))):
-            copy = pltpu.make_async_remote_copy(
-                src_ref=lost.at[field, pl.ds(start, HALO)],
-                dst_ref=lost.at[field, pl.ds(to, HALO)],
+        for way in range(2):
+            halo(field, way, "start")
+
+    def halo(field, way, action):
+        wrap, neighbour, first, to = wraps[way]
+
+        def copy():
+            return pltpu.make_async_remote_copy(
+                src_ref=lost.at[field, pl.ds(HALO + first, HALO)],
+                dst_ref=lost.at[field, pl.ds(first + to, HALO)],
                 send_sem=halo_send.at[field, way],
                 recv_sem=halo_recv.at[field, way],
                 device_id={"slab": neighbour},
                 device_id_type=MESH,
             )
-            copy.start()
-            halo_copies.append(copy)
-
+
+        if action == "start" or action == "sent":
+
+            @pl.when(jnp.logical_not(wrap))
+            def _():
+                copy().start() if action == "start" else copy().wait_send()
+
+        else:
+            far = wraps[1 - way][0]
+
+            @pl.when(jnp.logical_not(far))
+            def _():
+                copy().wait_recv()
+
+            @pl.when(far)
+            def _():
+                for layer in range(HALO):
+                    pltpu.make_async_remote_copy(
+                        src_ref=packed.at[field, 0],
+                        dst_ref=lost.at[field, first + to + layer],
+                        send_sem=wrap_send.at[field, 0],
+                        recv_sem=wrap_recv.at[field, way, layer],
+                        device_id={"slab": neighbour},
+                        device_id_type=MESH,
+                    ).wait_recv()
+
+    def between(step):
+        if step != 1:
+            pass_halos((2, None, 3, 4)[step])
+
+    pass_layers(0)
+    pass_layers(1)
+    pass_layers(2)
+    pass_halos(0)
+    pass_layers(3)
+    pass_halos(1)
+    pass_layers(4)
     live_in.wait()
     for copy in live_copies:
         copy.wait_recv()
-    run_sections(live, stencil(levels_ref, 1), to_advanced, pass_halos)
-    pass_halos(4)
+    run_sections(live, stencil(levels_ref, 1), to_advanced, between)
     lost_scalars = stencil(levels_ref, 0)
-    for copy in halo_copies:
-        copy.wait_recv()
+    for field in range(FIELDS):
+        for way in range(2):
+            halo(field, way, "received")
     run_sections(lost, lost_scalars, to_recovered, lambda step: None)
 
     recovered_out = pltpu.make_async_copy(recovered, recovered_ref, local_sem.at[0])
     recovered_out.start()
 
-    third_copies = []
-    for field in range(FIELDS):
-        for i, peer in enumerate(peers):
-            copy = pltpu.make_async_remote_copy(
-                src_ref=weighted.at[peer, field],
-                dst_ref=arrived.at[field, i],
-                send_sem=send3.at[field, i],
-                recv_sem=recv3.at[field, i],
-                device_id={"buddy": peer},
-                device_id_type=MESH,
-            )
-            copy.start()
-            third_copies.append(copy)
+    signs = (1, 3)
+    sides = [((row + sign) % 4) * 2 + half for sign in signs]
+    across = row * 2 + 1 - half
+    third_copies = {}
+
+    def send(field, message, source, target, peer):
+        copy = pltpu.make_async_remote_copy(
+            src_ref=source,
+            dst_ref=target,
+            send_sem=send3.at[field, message],
+            recv_sem=recv3.at[field, message],
+            device_id={"buddy": peer},
+            device_id_type=MESH,
+        )
+        copy.start()
+        third_copies[field, message] = copy
+
+    def rows(way):
+        return pl.ds(way * (CY // 2), CY // 2)
+
+    def start_along(field):
+        far = (row + 2) % 4
+        for way, sign in enumerate(signs):
+            near = (row + sign) % 4
+            send(field, way, weighted.at[far, way, field], far_in.at[way, field], sides[way])
+            send(field, 2 + way, weighted.at[near, 1 - way, field], near_in.at[way, field, 1 - way], sides[way])
+
+    def pass_along(field):
+        for way, sign in enumerate(signs):
+            near = (row + sign) % 4
+            third_copies[field, way].wait_recv()
+            near_out[way, field] = far_in[way, field] + weighted[near, way, field]
+            send(field, 4 + way, near_out.at[way, field], near_in.at[way, field, way], sides[way])
+
+    def finish_along(field):
+        for message in range(2, 6):
+            third_copies[field, message].wait_recv()
+
+        def column(layer):
+            return weighted[row, layer, field] + (near_in[0, field, layer] + near_in[1, field, layer])
+
+        across_out[field] = column(1 - half)
+        columns[field, 0] = column(half)
+        send(field, 6, across_out.at[field], across_in.at[field, 0], across)
+
+    def start_across(field):
+        send(field, 6, weighted.at[:, 1 - half, field], across_in.at[field], across)
+
+    def turn_across(field):
+        third_copies[field, 6].wait_recv()
+        for column in range(4):
+            columns[field, column] = weighted[column, half, field] + across_in[field, column]
+        far = (row + 2) % 4
+        for way, sign in enumerate(signs):
+            near = (row + sign) % 4
+            send(field, way, columns.at[field, far, rows(way)], far_in.at[way, field, rows(way)], sides[way])
+            send(
+                field,
+                2 + way,
+                columns.at[field, near, rows(1 - way)],
+                near_in.at[way, field, 0, rows(1 - way)],
+                sides[way],
+            )
+
+    def pass_across(field):
+        for way, sign in enumerate(signs):
+            near = (row + sign) % 4
+            third_copies[field, way].wait_recv()
+            near_out[way, field, rows(way)] = far_in[way, field, rows(way)] + columns[field, near, rows(way)]
+            send(
+                field,
+                4 + way,
+                near_out.at[way, field, rows(way)],
+                near_in.at[way, field, 0, rows(way)],
+                sides[way],
+            )
+
+    def whole_along(field):
+        third_copies[field, 6].wait_recv()
+        return columns[field, 0] + across_in[field, 0]
+
+    def whole_across(field):
+        for message in range(2, 6):
+            third_copies[field, message].wait_recv()
+        return columns[field, row] + (near_in[0, field, 0] + near_in[1, field, 0])
+
+    for step, fields in (
+        (start_across, ACROSS),
+        (start_along, ALONG),
+        (pass_along, ALONG),
+        (turn_across, ACROSS),
+        (finish_along, ALONG),
+        (pass_across, ACROSS),
+    ):
+        for field in fields:
+            step(field)
 
     for field in range(FIELDS):
         total[field, 16] = jnp.zeros((2, CX), jnp.float32)
     fourth_copies = []
-    for field in range(FIELDS):
-        summed = weighted[me, field]
-        for i in range(PEERS):
-            third_copies[field * PEERS + i].wait_recv()
-            summed = summed + arrived[field, i]
+    for field in ALONG + ACROSS:
+        summed = whole_along(field) if field in ALONG else whole_across(field)
         for tile in range(16):
             total[field, tile] = summed[2 * tile : 2 * tile + 2]
         for i, peer in enumerate(peers):
             for rank in range(4):
-                chosen[field, i, pl.ds(rank * 2, 2), :] = total[field, tiles_ref[peer * 4 + rank]]
+                chosen[field, i, rank] = total[field, numbers[8, peer * 4 + rank]]
             copy = pltpu.make_async_remote_copy(
                 src_ref=chosen.at[field, i],
-                dst_ref=combined_ref.at[field, me],
+                dst_ref=combined_ref.at[:, field, me],
                 send_sem=send4.at[field, i],
                 recv_sem=recv4.at[field, i],
                 device_id={"buddy": peer},
@@ -290,71 +468,113 @@
             copy.start()
             fourth_copies.append(copy)
         for rank in range(4):
-            combined_ref[field, me, pl.ds(rank * 2, 2), :] = total[field, tiles_ref[me * 4 + rank]]
-
+            combined_ref[rank, field, me] = total[field, numbers[8, me * 4 + rank]]
+
+    recovered_out.wait()
     for copy in fourth_copies:
         copy.wait()
-    for copy in first_copies + second_copies + third_copies + live_copies + halo_copies:
+    for copy in first_copies + second_copies + list(third_copies.values()) + live_copies:
         copy.wait_send()
-    recovered_out.wait()
+    for field in range(FIELDS):
+        for way in range(2):
+            halo(field, way, "sent")
+            for i in range(PEERS + 1):
+                wrapped(field, i, way, "sent")
+
+
+def hand_over(recovered, combined):
+    def copies(recovered_in, combined_in, recovered_out, combined_out, fields, tiles, sem_in, sem_out):
+        pairs = [
+            (recovered_in.at[0, field], fields.at[field], recovered_out.at[0, field]) for field in range(FIELDS)
+        ] + [(combined_in, tiles, combined_out)]
+        first = [
+            pltpu.make_async_copy(pair[0], pair[1], sem_in.at[i]) for i, pair in enumerate(pairs)
+        ]
+        second = [
+            pltpu.make_async_copy(pair[1], pair[2], sem_out.at[i]) for i, pair in enumerate(pairs)
+        ]
+        for copy in first:
+            copy.start()
+        for before, after in zip(first, second):
+            before.wait()
+            after.start()
+        for copy in second:
+            copy.wait()
+
+    away = pl.BlockSpec(memory_space=pltpu.HBM)
+    return pl.pallas_call(
+        copies,
+        name="hand_over",
+        out_shape=(
+            jax.ShapeDtypeStruct(recovered.shape, recovered.dtype),
+            jax.ShapeDtypeStruct(combined.shape, combined.dtype),
+        ),
+        in_specs=[away, away],
+        out_specs=(away, away),
+        scratch_shapes=[
+            pltpu.VMEM(recovered.shape[1:], jnp.float32),
+            pltpu.VMEM(combined.shape, jnp.float32),
+            pltpu.SemaphoreType.DMA((FIELDS + 1,)),
+            pltpu.SemaphoreType.DMA((FIELDS + 1,)),
+        ],
+        compiler_params=pltpu.CompilerParams(vmem_limit_bytes=63 << 20),
+    )(recovered, combined)
 
 
 def body(checkpoint, slot_block, live_state, levels, coefficients, tile_owner):
-    ids = jnp.arange(64, dtype=jnp.int32)
-    inverse = jnp.sum(jnp.where(slot_block.reshape(1, 64) == ids[:, None], ids[None, :], 0), axis=1)
-    owners = tile_owner[0]
-    order = jnp.arange(16, dtype=jnp.int32)
-    ranks = jnp.sum(
-        jnp.where((owners[None, :] == owners[:, None]) & (order[None, :] < order[:, None]), 1, 0), axis=1
-    )
-    slots = owners * 4 + ranks
-    seats = jnp.arange(32, dtype=jnp.int32)
-    tiles = 16 + jnp.sum(jnp.where(slots[None, :] == seats[:, None], order[None, :] - 16, 0), axis=1)
     smem = pl.BlockSpec(memory_space=pltpu.SMEM)
-    away = pl.BlockSpec(memory_space=pl.ANY)
+    away = pl.BlockSpec(memory_space=pltpu.HBM)
     dma = pltpu.SemaphoreType.DMA
     recovered, combined = pl.pallas_call(
         kernel,
         name="recover_and_combine",
         out_shape=(
             jax.ShapeDtypeStruct((FIELDS, CZ, CY, CX), jnp.float32),
-            jax.ShapeDtypeStruct((FIELDS, CZ, 8, CX), jnp.float32),
+            jax.ShapeDtypeStruct((4, FIELDS, CZ, 2, CX), jnp.float32),
         ),
         in_specs=[smem, smem, smem, smem, away, away],
         out_specs=(away, pl.BlockSpec(memory_space=pltpu.VMEM)),
         scratch_shapes=[
             *[pltpu.VMEM((64, 4, CX), jnp.float32) for _ in range(FIELDS)],
-            pltpu.VMEM((FIELDS, PEERS, CY, CX), jnp.float32),
+            pltpu.VMEM((FIELDS, PEERS + 1, CY, CX), jnp.float32),
             pltpu.VMEM((FIELDS, CZ + 2 * HALO, CY, CX), jnp.float32),
             pltpu.VMEM((FIELDS, CZ + 2 * HALO, CY, CX), jnp.float32),
             pltpu.VMEM((FIELDS, CZ + 2 * HALO, CY, CX), jnp.float32),
             pltpu.VMEM((FIELDS, CZ + 2 * HALO, CY, CX), jnp.float32),
             pltpu.VMEM((CZ, FIELDS, CY, CX), jnp.float32),
             pltpu.VMEM((FIELDS, CZ, CY, CX), jnp.float32),
-            pltpu.VMEM((CZ, FIELDS, CY, CX), jnp.float32),
-            pltpu.VMEM((FIELDS, PEERS, CY, CX), jnp.float32),
+            pltpu.VMEM((4, 2, FIELDS, CY, CX), jnp.float32),
+            pltpu.VMEM((2, FIELDS, CY, CX), jnp.float32),
+            pltpu.VMEM((2, FIELDS, CY, CX), jnp.float32),
+            pltpu.VMEM((2, FIELDS, 2, CY, CX), jnp.float32),
+            pltpu.VMEM((FIELDS, CY, CX), jnp.float32),
+            pltpu.VMEM((FIELDS, 4, CY, CX), jnp.float32),
+            pltpu.VMEM((FIELDS, 4, CY, CX), jnp.float32),
             pltpu.VMEM((FIELDS, 17, 2, CX), jnp.float32),
-            pltpu.VMEM((FIELDS, PEERS, 8, CX), jnp.float32),
-            dma((1 + FIELDS,)),
-            dma((FIELDS, PEERS)),
-            dma((FIELDS, PEERS)),
-            dma((FIELDS, PEERS)),
-            dma((FIELDS, PEERS)),
-            dma((FIELDS, PEERS)),
-            dma((FIELDS, PEERS)),
-            dma((FIELDS, PEERS)),
-            dma((FIELDS, PEERS)),
+            pltpu.VMEM((FIELDS, PEERS, 4, 2, CX), jnp.float32),
+            pltpu.VMEM((16, 128), jnp.int32),
+            pltpu.SMEM((16, 128), jnp.int32),
+            dma((2 + FIELDS,)),
+            dma((FIELDS, PEERS)),
+            dma((FIELDS, PEERS)),
+            dma((FIELDS, PEERS)),
+            dma((FIELDS, PEERS)),
+            dma((FIELDS, PEERS)),
+            dma((FIELDS, PEERS)),
+            dma((FIELDS, PEERS)),
+            dma((FIELDS, PEERS)),
+            dma((FIELDS, PEERS + 1)),
+            dma((FIELDS, 2, HALO)),
             dma((FIELDS, 2)),
             dma((FIELDS, 2)),
             dma((2,)),
             dma((2,)),
         ],
         compiler_params=pltpu.CompilerParams(
-            collective_id=0, has_side_effects=True, vmem_limit_bytes=48 << 20
+            collective_id=0, has_side_effects=True, vmem_limit_bytes=63 << 20
         ),
-    )(inverse, tiles, levels, coefficients, checkpoint, live_state)
-    combined = combined.reshape(FIELDS, CZ, 4, 2, CX).transpose(2, 0, 1, 3, 4)
-    return recovered[None], combined
+    )(slot_block, tile_owner, levels, coefficients.reshape(1, 2), checkpoint, live_state)
+    return hand_over(recovered[None], combined)
 
 
 def solution(mesh):

time: 98.2 us -> 90.4 us (0.921)
  local copies, waits for them, and re-layouts: 6.96 us -> 0 us
  other arithmetic: 1.79 us -> 0 us
  Pallas kernels: 87.2 us -> 88.5 us
    unnamed x8 -> x0, local copies, waits for them, and re-layouts: 5.11 us -> none
    pallas_call x0 -> x1, Pallas kernels: none -> 2.21 us  [hand_over(): pl.pallas_call(copies, name='hand_over', out_shape=(jax.ShapeDtypeStruct(...]
    reduce_sum x3 -> x0, other arithmetic: 1.12 us -> none  [the longest x1 0.92 us: body(): jnp.sum(jnp.where((owners[None, :] == owners[:, None]) & (order[None, :]...]
    reshape x2 -> x0, local copies, waits for them, and re-layouts: 1.09 us -> none  [body(): combined = combined.reshape(FIELDS, CZ, 4, 2, CX).transpose(2, 0, 1, 3, 4)]
where the time goes in v1:
time: 90.4 us; the launch traced here: 89.2 us
  Pallas kernels  88.5 us (98%)
    pallas_call x1, Pallas kernels, body(): pl.pallas_call(kernel, name='recover_and_combine', out_shape=(jax.ShapeDt...  86.3 us
    pallas_call x1, Pallas kernels, hand_over(): pl.pallas_call(copies, name='hand_over', out_shape=(jax.ShapeDtypeStruct(...  2.21 us

profile of v1, /device:TPU:7, one launch (start us, length us, event | category | flops | bytes accessed | tf_op | source)
XLA Modules:
  0.0 89.2 jit_solution(16996128886038979051)
XLA Ops:
  0.6 86.3 %recover_and_combine.1 = (f32[5,8,32,256]{3,2,1,0:T(8,128)}, f32[4,5,8,2,256]{4,3,2,1,0:T(2,128)}) custom-call(s32[8,8]{1,0:T(8,128)} %slots_ref.1, s32[1,16]{1,0:T(1,128)} %owners_ref.1, s32[2,1,3]{2,1,0:T(1,128)} %levels_ref.1, f32[1,2]{1,0:T(1,128)} %bitcast.3, f32[8,5,8,4,256]{4,3,2,1,0:T(4,128)} %checkpoint_ref.1, f32[1,5,8,32,256]{4,3,2,1,0:T(8,128)} %live_ref.1), custom_call_target="tpu_custom_call" | custom-call | tf_op jit(solution)/shard_map/recover_and_combine/pallas_call | solution.py:528
  87.0 2.2 %hand_over.1 = (f32[1,5,8,32,256]{4,3,2,1,0:T(8,128)}, f32[4,5,8,2,256]{4,3,2,1,0:T(2,128)}) custom-call(f32[1,5,8,32,256]{4,3,2,1,0:T(8,128)} %bitcast.2, f32[4,5,8,2,256]{4,3,2,1,0:T(2,128)} %get-tuple-element.5.combined_in), custom_call_target="tpu_custom_call" | custom-call | tf_op jit(solution)/shard_map/hand_over/pallas_call | solution.py:505

commit v2 on v1

--- a/solution.py
+++ b/solution.py
@@ -15,8 +15,6 @@
 CX = 256
 HALO = 4
 PEERS = 7
-ALONG = (0, 1, 2)
-ACROSS = (3, 4)
 OFFSETS = ((2, 1), (2, 0), (1, 1), (3, 1), (0, 1), (1, 0), (3, 0))
 
 
@@ -97,15 +95,12 @@
     live,
     stage_a,
     stage_b,
+    live_a,
+    live_b,
     advanced,
     recovered,
     weighted,
-    far_in,
-    near_out,
-    near_in,
-    across_out,
-    across_in,
-    columns,
+    arrived,
     total,
     chosen,
     tables,
@@ -182,18 +177,27 @@
             )
             copy.start()
             first_copies.append(copy)
-    live_copies = []
-    for way, (neighbour, start, to) in enumerate(((below, 0, HALO + CZ), (above, CZ - HALO, 0))):
-        copy = pltpu.make_async_remote_copy(
-            src_ref=live_ref.at[0, :, pl.ds(start, HALO)],
-            dst_ref=live.at[:, pl.ds(to, HALO)],
+
+    def live_copy(way):
+        _, neighbour, first, to = wraps[way]
+        return pltpu.make_async_remote_copy(
+            src_ref=live_ref.at[0, :, pl.ds(first, HALO)],
+            dst_ref=live.at[:, pl.ds(first + to, HALO)],
             send_sem=live_send.at[way],
             recv_sem=live_recv.at[way],
             device_id={"slab": neighbour},
             device_id_type=MESH,
         )
-        copy.start()
-        live_copies.append(copy)
+
+    def start_live(across_the_slice):
+        for way in range(2):
+            wrap = wraps[way][0]
+
+            @pl.when(wrap if across_the_slice else jnp.logical_not(wrap))
+            def _():
+                live_copy(way).start()
+
+    start_live(False)
 
     lanes = lax.broadcasted_iota(jnp.int32, (8, 128), 1)
     held_in = jnp.zeros((8, 128), jnp.int32)
@@ -272,15 +276,17 @@
             recovered[field, z - HALO] = results[field]
             weighted[(z - HALO) // 2, (z - HALO) % 2, field] = share * results[field] + live_share * advanced[z - HALO, field]
 
-    def run_sections(state, scalars, finish, between):
+    def to_weighted(z, results):
+        for field in range(FIELDS):
+            weighted[(z - HALO) // 2, (z - HALO) % 2, field] = (
+                share * recovered[field, z - HALO] + live_share * results[field]
+            )
+
+    def run_sections(state, scalars, finish):
         section(state, state, scalars, 0.25, 1, 2 * HALO + CZ - 1, to_buffer(stage_a))
-        between(0)
         section(stage_a, state, scalars, 1.0 / 3.0, 2, 2 * HALO + CZ - 2, to_buffer(stage_b))
-        between(1)
         section(stage_b, state, scalars, 0.5, 3, 2 * HALO + CZ - 3, to_buffer(stage_a))
-        between(2)
         section(stage_a, state, scalars, 1.0, HALO, HALO + CZ, finish)
-        between(3)
 
     def pass_halos(field):
         for i in range(PEERS):
@@ -326,9 +332,46 @@
                         device_id_type=MESH,
                     ).wait_recv()
 
-    def between(step):
-        if step != 1:
-            pass_halos((2, None, 3, 4)[step])
+    live_scalars = stencil(levels_ref, 1)
+    lost_scalars = stencil(levels_ref, 0)
+    last = 2 * HALO + CZ
+
+    def live_section(step, spans, finish):
+        source, share_of_step, write = (
+            (live, 0.25, to_buffer(live_a)),
+            (live_a, 1.0 / 3.0, to_buffer(live_b)),
+            (live_b, 0.5, to_buffer(live_a)),
+            (live_a, 1.0, finish),
+        )[step]
+        for first, end in spans:
+            section(source, live, live_scalars, share_of_step, first, end, write)
+
+    def early_live(step):
+        @pl.when(jnp.logical_not(crossing))
+        def _():
+            if step == 0:
+                for way in range(2):
+                    live_copy(way).wait_recv()
+            live_section(step, ((1 + step, last - 1 - step),), to_advanced)
+
+        if step < 3:
+
+            @pl.when(crossing)
+            def _():
+                live_section(step, ((HALO + 1 + step, HALO + CZ - 1 - step),), None)
+
+    def late_live():
+        @pl.when(crossing)
+        def _():
+            for way in range(2):
+                live_copy(way).wait_recv()
+            for step in range(3):
+                live_section(
+                    step,
+                    ((1 + step, HALO + 1 + step), (HALO + CZ - 1 - step, last - 1 - step)),
+                    None,
+                )
+            live_section(3, ((HALO, HALO + CZ),), to_weighted)
 
     pass_layers(0)
     pass_layers(1)
@@ -338,120 +381,45 @@
     pass_halos(1)
     pass_layers(4)
     live_in.wait()
-    for copy in live_copies:
-        copy.wait_recv()
-    run_sections(live, stencil(levels_ref, 1), to_advanced, between)
-    lost_scalars = stencil(levels_ref, 0)
+    early_live(0)
+    pass_halos(2)
+    early_live(1)
+    early_live(2)
+    pass_halos(3)
+    early_live(3)
+    pass_halos(4)
+    start_live(True)
     for field in range(FIELDS):
         for way in range(2):
             halo(field, way, "received")
-    run_sections(lost, lost_scalars, to_recovered, lambda step: None)
+    run_sections(lost, lost_scalars, to_recovered)
+    late_live()
 
     recovered_out = pltpu.make_async_copy(recovered, recovered_ref, local_sem.at[0])
     recovered_out.start()
 
-    signs = (1, 3)
-    sides = [((row + sign) % 4) * 2 + half for sign in signs]
-    across = row * 2 + 1 - half
     third_copies = {}
-
-    def send(field, message, source, target, peer):
-        copy = pltpu.make_async_remote_copy(
-            src_ref=source,
-            dst_ref=target,
-            send_sem=send3.at[field, message],
-            recv_sem=recv3.at[field, message],
-            device_id={"buddy": peer},
-            device_id_type=MESH,
-        )
-        copy.start()
-        third_copies[field, message] = copy
-
-    def rows(way):
-        return pl.ds(way * (CY // 2), CY // 2)
-
-    def start_along(field):
-        far = (row + 2) % 4
-        for way, sign in enumerate(signs):
-            near = (row + sign) % 4
-            send(field, way, weighted.at[far, way, field], far_in.at[way, field], sides[way])
-            send(field, 2 + way, weighted.at[near, 1 - way, field], near_in.at[way, field, 1 - way], sides[way])
-
-    def pass_along(field):
-        for way, sign in enumerate(signs):
-            near = (row + sign) % 4
-            third_copies[field, way].wait_recv()
-            near_out[way, field] = far_in[way, field] + weighted[near, way, field]
-            send(field, 4 + way, near_out.at[way, field], near_in.at[way, field, way], sides[way])
-
-    def finish_along(field):
-        for message in range(2, 6):
-            third_copies[field, message].wait_recv()
-
-        def column(layer):
-            return weighted[row, layer, field] + (near_in[0, field, layer] + near_in[1, field, layer])
-
-        across_out[field] = column(1 - half)
-        columns[field, 0] = column(half)
-        send(field, 6, across_out.at[field], across_in.at[field, 0], across)
-
-    def start_across(field):
-        send(field, 6, weighted.at[:, 1 - half, field], across_in.at[field], across)
-
-    def turn_across(field):
-        third_copies[field, 6].wait_recv()
-        for column in range(4):
-            columns[field, column] = weighted[column, half, field] + across_in[field, column]
-        far = (row + 2) % 4
-        for way, sign in enumerate(signs):
-            near = (row + sign) % 4
-            send(field, way, columns.at[field, far, rows(way)], far_in.at[way, field, rows(way)], sides[way])
-            send(
-                field,
-                2 + way,
-                columns.at[field, near, rows(1 - way)],
-                near_in.at[way, field, 0, rows(1 - way)],
-                sides[way],
-            )
-
-    def pass_across(field):
-        for way, sign in enumerate(signs):
-            near = (row + sign) % 4
-            third_copies[field, way].wait_recv()
-            near_out[way, field, rows(way)] = far_in[way, field, rows(way)] + columns[field, near, rows(way)]
-            send(
-                field,
-                4 + way,
-                near_out.at[way, field, rows(way)],
-                near_in.at[way, field, 0, rows(way)],
-                sides[way],
-            )
-
-    def whole_along(field):
-        third_copies[field, 6].wait_recv()
-        return columns[field, 0] + across_in[field, 0]
-
-    def whole_across(field):
-        for message in range(2, 6):
-            third_copies[field, message].wait_recv()
-        return columns[field, row] + (near_in[0, field, 0] + near_in[1, field, 0])
-
-    for step, fields in (
-        (start_across, ACROSS),
-        (start_along, ALONG),
-        (pass_along, ALONG),
-        (turn_across, ACROSS),
-        (finish_along, ALONG),
-        (pass_across, ACROSS),
-    ):
-        for field in fields:
-            step(field)
+    for field in range(FIELDS):
+        for i, peer in enumerate(peers):
+            copy = pltpu.make_async_remote_copy(
+                src_ref=weighted.at[peer // 2, peer % 2, field],
+                dst_ref=arrived.at[field, i],
+                send_sem=send3.at[field, i],
+                recv_sem=recv3.at[field, i],
+                device_id={"buddy": peer},
+                device_id_type=MESH,
+            )
+            copy.start()
+            third_copies[field, i] = copy
 
     for field in range(FIELDS):
         total[field, 16] = jnp.zeros((2, CX), jnp.float32)
     fourth_copies = []
-    for field in ALONG + ACROSS:
-        summed = whole_along(field) if field in ALONG else whole_across(field)
+    for field in range(FIELDS):
+        summed = weighted[row, half, field]
+        for i in range(PEERS):
+            third_copies[field, i].wait_recv()
+            summed = summed + arrived[field, i]
         for tile in range(16):
             total[field, tile] = summed[2 * tile : 2 * tile + 2]
         for i, peer in enumerate(peers):
@@ -473,8 +441,10 @@
     recovered_out.wait()
     for copy in fourth_copies:
         copy.wait()
-    for copy in first_copies + second_copies + list(third_copies.values()) + live_copies:
+    for copy in first_copies + second_copies + list(third_copies.values()):
         copy.wait_send()
+    for way in range(2):
+        live_copy(way).wait_send()
     for field in range(FIELDS):
         for way in range(2):
             halo(field, way, "sent")
@@ -541,15 +511,12 @@
             pltpu.VMEM((FIELDS, CZ + 2 * HALO, CY, CX), jnp.float32),
             pltpu.VMEM((FIELDS, CZ + 2 * HALO, CY, CX), jnp.float32),
             pltpu.VMEM((FIELDS, CZ + 2 * HALO, CY, CX), jnp.float32),
+            pltpu.VMEM((FIELDS, CZ + 2 * HALO, CY, CX), jnp.float32),
+            pltpu.VMEM((FIELDS, CZ + 2 * HALO, CY, CX), jnp.float32),
             pltpu.VMEM((CZ, FIELDS, CY, CX), jnp.float32),
             pltpu.VMEM((FIELDS, CZ, CY, CX), jnp.float32),
             pltpu.VMEM((4, 2, FIELDS, CY, CX), jnp.float32),
-            pltpu.VMEM((2, FIELDS, CY, CX), jnp.float32),
-            pltpu.VMEM((2, FIELDS, CY, CX), jnp.float32),
-            pltpu.VMEM((2, FIELDS, 2, CY, CX), jnp.float32),
-            pltpu.VMEM((FIELDS, CY, CX), jnp.float32),
-            pltpu.VMEM((FIELDS, 4, CY, CX), jnp.float32),
-            pltpu.VMEM((FIELDS, 4, CY, CX), jnp.float32),
+            pltpu.VMEM((FIELDS, PEERS, CY, CX), jnp.float32),
             pltpu.VMEM((FIELDS, 17, 2, CX), jnp.float32),
             pltpu.VMEM((FIELDS, PEERS, 4, 2, CX), jnp.float32),
             pltpu.VMEM((16, 128), jnp.int32),

time: 90.4 us -> 85.7 us (0.948)
  Pallas kernels: 88.5 us -> 83.9 us
    pallas_call x1, Pallas kernels: 86.3 us -> 81.7 us  [body(): pl.pallas_call(kernel, name='recover_and_combine', out_shape=(jax.ShapeDt...]
where the time goes in v2:
time: 85.7 us; the launch traced here: 84.6 us
  Pallas kernels  83.9 us (98%)
    pallas_call x1, Pallas kernels, body(): pl.pallas_call(kernel, name='recover_and_combine', out_shape=(jax.ShapeDt...  81.7 us
    pallas_call x1, Pallas kernels, hand_over(): pl.pallas_call(copies, name='hand_over', out_shape=(jax.ShapeDtypeStruct(...  2.21 us

profile of v2, /device:TPU:7, one launch (start us, length us, event | category | flops | bytes accessed | tf_op | source)
XLA Modules:
  0.0 84.6 jit_solution(5004991741104428026)
XLA Ops:
  0.6 81.7 %recover_and_combine.1 = (f32[5,8,32,256]{3,2,1,0:T(8,128)}, f32[4,5,8,2,256]{4,3,2,1,0:T(2,128)}) custom-call(s32[8,8]{1,0:T(8,128)} %slots_ref.1, s32[1,16]{1,0:T(1,128)} %owners_ref.1, s32[2,1,3]{2,1,0:T(1,128)} %levels_ref.1, f32[1,2]{1,0:T(1,128)} %bitcast.3, f32[8,5,8,4,256]{4,3,2,1,0:T(4,128)} %checkpoint_ref.1, f32[1,5,8,32,256]{4,3,2,1,0:T(8,128)} %live_ref.1), custom_call_target="tpu_custom_call" | custom-call | tf_op jit(solution)/shard_map/recover_and_combine/pallas_call | solution.py:498
  82.4 2.2 %hand_over.1 = (f32[1,5,8,32,256]{4,3,2,1,0:T(8,128)}, f32[4,5,8,2,256]{4,3,2,1,0:T(2,128)}) custom-call(f32[1,5,8,32,256]{4,3,2,1,0:T(8,128)} %bitcast.2, f32[4,5,8,2,256]{4,3,2,1,0:T(2,128)} %get-tuple-element.5.combined_in), custom_call_target="tpu_custom_call" | custom-call | tf_op jit(solution)/shard_map/hand_over/pallas_call | solution.py:475

commit v3 on v2

--- a/solution.py
+++ b/solution.py
@@ -41,39 +41,71 @@
     return middle, sides
 
 
-def section(source, base, scalars, share, first, last, write):
+def section(source, base, scalars, share, first, last, write, entry=False):
     middle, sides = scalars
     middle = middle * share
     sides = [tuple(value * share for value in side) for side in sides]
+    pairs = [
+        (
+            (0.5 * (side[0] + side[2]), 0.5 * (side[1] - side[2])),
+            (0.5 * (side[0] - side[2]), 0.5 * (side[1] + side[2])),
+        )
+        for side in sides
+    ]
+    turns = ((1, CX), (0, CY))
+
+    def turned(axis, q):
+        dim, size = turns[axis]
+        return (lambda: pltpu.roll(q, size - 1, dim), lambda: pltpu.roll(q, 1, dim))
 
     def one_layer(z, carry):
-        def own_terms(field):
-            q = source[field, z]
-            out = base[field, z] + middle * q
-            shifted = (
-                (pltpu.roll(q, CX - 1, 1), pltpu.roll(q, 1, 1)),
-                (pltpu.roll(q, CY - 1, 0), pltpu.roll(q, 1, 0)),
-                (source[field, z + 1], source[field, z - 1]),
-            )
-            for (plus, minus), side in zip(shifted, sides):
-                out = out + (side[0] * plus + side[1] * minus)
-            return out, shifted
-
-        pressure, around = own_terms(4)
-        pushes = [side[2] * (plus - minus) for (plus, minus), side in zip(around, sides)]
-        spread = None
+        pressure = source[4, z]
+        speeds = [source[1 + axis, z] for axis in range(3)]
+        pressure_out = base[4, z] + middle * pressure
         results = [None] * FIELDS
         for axis in range(3):
-            out, around = own_terms(1 + axis)
-            results[1 + axis] = out + pushes[axis]
-            part = sides[axis][2] * (around[axis][0] - around[axis][1])
-            spread = part if spread is None else spread + part
-        results[4] = pressure + spread
-        results[0] = own_terms(0)[0] + spread
+            if axis < 2:
+                sums = turned(axis, pressure + speeds[axis])
+                gaps = turned(axis, pressure - speeds[axis])
+            else:
+                up, down = (source[4, z + 1], source[3, z + 1]), (source[4, z - 1], source[3, z - 1])
+                sums = (lambda: up[0] + up[1], lambda: down[0] + down[1])
+                gaps = (lambda: up[0] - up[1], lambda: down[0] - down[1])
+            if VELOCITY[axis] > 0:
+                right = pairs[axis][0][1] * sums[1]()
+                left = pairs[axis][1][0] * gaps[0]() + pairs[axis][1][1] * gaps[1]()
+            else:
+                right = pairs[axis][0][0] * sums[0]() + pairs[axis][0][1] * sums[1]()
+                left = pairs[axis][1][0] * gaps[0]()
+            pressure_out = pressure_out + (right + left)
+            out = base[1 + axis, z] + middle * speeds[axis]
+            out = out + (right - left)
+            for other in range(3):
+                if other != axis:
+                    if other < 2:
+                        plus, minus = (side() for side in turned(other, speeds[axis]))
+                    else:
+                        plus, minus = source[1 + axis, z + 1], source[1 + axis, z - 1]
+                    out = out + (sides[other][0] * plus + sides[other][1] * minus)
+            results[1 + axis] = out
+        results[4] = pressure_out
+
+        def excess(at):
+            return source[0, at] - source[4, at] if entry else source[0, at]
+
+        q = source[0, z] - pressure if entry else source[0, z]
+        out = (q if entry else base[0, z] - base[4, z]) + middle * q
+        for axis in range(3):
+            if axis < 2:
+                plus, minus = (side() for side in turned(axis, q))
+            else:
+                plus, minus = excess(z + 1), excess(z - 1)
+            out = out + (sides[axis][0] * plus + sides[axis][1] * minus)
+        results[0] = out
         write(z, results)
         return carry
 
-    lax.fori_loop(first, last, one_layer, 0)
+    lax.fori_loop(first, last, one_layer, 0, unroll=2)
 
 
 def kernel(
@@ -265,6 +297,7 @@
         return write
 
     def to_advanced(z, results):
+        results = [results[0] + results[4]] + results[1:]
         for field in range(FIELDS):
             advanced[z - HALO, field] = results[field]
 
@@ -272,18 +305,20 @@
     live_share = coefficients_ref[0, 1]
 
     def to_recovered(z, results):
+        results = [results[0] + results[4]] + results[1:]
         for field in range(FIELDS):
             recovered[field, z - HALO] = results[field]
             weighted[(z - HALO) // 2, (z - HALO) % 2, field] = share * results[field] + live_share * advanced[z - HALO, field]
 
     def to_weighted(z, results):
+        results = [results[0] + results[4]] + results[1:]
         for field in range(FIELDS):
             weighted[(z - HALO) // 2, (z - HALO) % 2, field] = (
                 share * recovered[field, z - HALO] + live_share * results[field]
             )
 
     def run_sections(state, scalars, finish):
-        section(state, state, scalars, 0.25, 1, 2 * HALO + CZ - 1, to_buffer(stage_a))
+        section(state, state, scalars, 0.25, 1, 2 * HALO + CZ - 1, to_buffer(stage_a), entry=True)
         section(stage_a, state, scalars, 1.0 / 3.0, 2, 2 * HALO + CZ - 2, to_buffer(stage_b))
         section(stage_b, state, scalars, 0.5, 3, 2 * HALO + CZ - 3, to_buffer(stage_a))
         section(stage_a, state, scalars, 1.0, HALO, HALO + CZ, finish)
@@ -344,7 +379,7 @@
             (live_a, 1.0, finish),
         )[step]
         for first, end in spans:
-            section(source, live, live_scalars, share_of_step, first, end, write)
+            section(source, live, live_scalars, share_of_step, first, end, write, entry=step == 0)
 
     def early_live(step):
         @pl.when(jnp.logical_not(crossing))
@@ -387,8 +422,8 @@
     early_live(2)
     pass_halos(3)
     early_live(3)
+    start_live(True)
     pass_halos(4)
-    start_live(True)
     for field in range(FIELDS):
         for way in range(2):
             halo(field, way, "received")

time: 85.7 us -> 83.4 us (0.973)
  Pallas kernels: 83.9 us -> 82.5 us
    pallas_call x1, Pallas kernels: 81.7 us -> 80.3 us  [body(): pl.pallas_call(kernel, name='recover_and_combine', out_shape=(jax.ShapeDt...]
where the time goes in v3:
time: 83.4 us; the launch traced here: 83.1 us
  Pallas kernels  82.5 us (99%)
    pallas_call x1, Pallas kernels, body(): pl.pallas_call(kernel, name='recover_and_combine', out_shape=(jax.ShapeDt...  80.3 us
    pallas_call x1, Pallas kernels, hand_over(): pl.pallas_call(copies, name='hand_over', out_shape=(jax.ShapeDtypeStruct(...  2.21 us

profile of v3, /device:TPU:7, one launch (start us, length us, event | category | flops | bytes accessed | tf_op | source)
XLA Modules:
  0.0 83.1 jit_solution(13896576436061531889)
XLA Ops:
  0.6 80.3 %recover_and_combine.1 = (f32[5,8,32,256]{3,2,1,0:T(8,128)}, f32[4,5,8,2,256]{4,3,2,1,0:T(2,128)}) custom-call(s32[8,8]{1,0:T(8,128)} %slots_ref.1, s32[1,16]{1,0:T(1,128)} %owners_ref.1, s32[2,1,3]{2,1,0:T(1,128)} %levels_ref.1, f32[1,2]{1,0:T(1,128)} %bitcast.3, f32[8,5,8,4,256]{4,3,2,1,0:T(4,128)} %checkpoint_ref.1, f32[1,5,8,32,256]{4,3,2,1,0:T(8,128)} %live_ref.1), custom_call_target="tpu_custom_call" | custom-call | tf_op jit(solution)/shard_map/recover_and_combine/pallas_call | solution.py:533
  80.9 2.2 %hand_over.1 = (f32[1,5,8,32,256]{4,3,2,1,0:T(8,128)}, f32[4,5,8,2,256]{4,3,2,1,0:T(2,128)}) custom-call(f32[1,5,8,32,256]{4,3,2,1,0:T(8,128)} %bitcast.2, f32[4,5,8,2,256]{4,3,2,1,0:T(2,128)} %get-tuple-element.5.combined_in), custom_call_target="tpu_custom_call" | custom-call | tf_op jit(solution)/shard_map/hand_over/pallas_call | solution.py:510

commit v4 on v3

--- a/solution.py
+++ b/solution.py
@@ -15,7 +15,7 @@
 CX = 256
 HALO = 4
 PEERS = 7
-OFFSETS = ((2, 1), (2, 0), (1, 1), (3, 1), (0, 1), (1, 0), (3, 0))
+OFFSETS = ((2, 1), (1, 1), (3, 1), (0, 1), (2, 0), (1, 0), (3, 0))
 
 
 def stencil(levels_ref, kind):
@@ -41,7 +41,7 @@
     return middle, sides
 
 
-def section(source, base, scalars, share, first, last, write, entry=False):
+def section(source, base, scalars, share, first, count, write, entry=False):
     middle, sides = scalars
     middle = middle * share
     sides = [tuple(value * share for value in side) for side in sides]
@@ -58,7 +58,8 @@
         dim, size = turns[axis]
         return (lambda: pltpu.roll(q, size - 1, dim), lambda: pltpu.roll(q, 1, dim))
 
-    def one_layer(z, carry):
+    def one_layer(i, carry):
+        z = first + i
         pressure = source[4, z]
         speeds = [source[1 + axis, z] for axis in range(3)]
         pressure_out = base[4, z] + middle * pressure
@@ -105,7 +106,7 @@
         write(z, results)
         return carry
 
-    lax.fori_loop(first, last, one_layer, 0, unroll=2)
+    lax.fori_loop(0, count, one_layer, 0, unroll=2)
 
 
 def kernel(
@@ -318,10 +319,10 @@
             )
 
     def run_sections(state, scalars, finish):
-        section(state, state, scalars, 0.25, 1, 2 * HALO + CZ - 1, to_buffer(stage_a), entry=True)
-        section(stage_a, state, scalars, 1.0 / 3.0, 2, 2 * HALO + CZ - 2, to_buffer(stage_b))
-        section(stage_b, state, scalars, 0.5, 3, 2 * HALO + CZ - 3, to_buffer(stage_a))
-        section(stage_a, state, scalars, 1.0, HALO, HALO + CZ, finish)
+        section(state, state, scalars, 0.25, 1, 2 * HALO + CZ - 2, to_buffer(stage_a), entry=True)
+        section(stage_a, state, scalars, 1.0 / 3.0, 2, 2 * HALO + CZ - 4, to_buffer(stage_b))
+        section(stage_b, state, scalars, 0.5, 3, 2 * HALO + CZ - 6, to_buffer(stage_a))
+        section(stage_a, state, scalars, 1.0, HALO, CZ, finish)
 
     def pass_halos(field):
         for i in range(PEERS):
@@ -369,44 +370,47 @@
 
     live_scalars = stencil(levels_ref, 1)
     lost_scalars = stencil(levels_ref, 0)
-    last = 2 * HALO + CZ
-
-    def live_section(step, spans, finish):
+
+    def live_section(step, first, count, finish):
         source, share_of_step, write = (
             (live, 0.25, to_buffer(live_a)),
             (live_a, 1.0 / 3.0, to_buffer(live_b)),
             (live_b, 0.5, to_buffer(live_a)),
             (live_a, 1.0, finish),
         )[step]
-        for first, end in spans:
-            section(source, live, live_scalars, share_of_step, first, end, write, entry=step == 0)
+        section(source, live, live_scalars, share_of_step, first, count, write, entry=step == 0)
+
+    late_below = slab % 8 == 0
+
+    def live_received(late):
+        for way in range(2):
+            far = wraps[1 - way][0]
+
+            @pl.when(far if late else jnp.logical_not(far))
+            def _():
+                live_copy(way).wait_recv()
 
     def early_live(step):
+        if step == 0:
+            live_received(False)
+
         @pl.when(jnp.logical_not(crossing))
         def _():
-            if step == 0:
-                for way in range(2):
-                    live_copy(way).wait_recv()
-            live_section(step, ((1 + step, last - 1 - step),), to_advanced)
-
-        if step < 3:
-
-            @pl.when(crossing)
-            def _():
-                live_section(step, ((HALO + 1 + step, HALO + CZ - 1 - step),), None)
-
-    def late_live():
+            live_section(step, 1 + step, 2 * HALO + CZ - 2 - 2 * step, to_advanced)
+
         @pl.when(crossing)
         def _():
-            for way in range(2):
-                live_copy(way).wait_recv()
-            for step in range(3):
-                live_section(
-                    step,
-                    ((1 + step, HALO + 1 + step), (HALO + CZ - 1 - step, last - 1 - step)),
-                    None,
-                )
-            live_section(3, ((HALO, HALO + CZ),), to_weighted)
+            first = jnp.where(late_below, HALO + 1 + step, 1 + step)
+            live_section(step, first, HALO + CZ - 2 - 2 * step, to_advanced)
+
+    def late_live():
+        live_received(True)
+
+        @pl.when(crossing)
+        def _():
+            for step in range(4):
+                first = jnp.where(late_below, 1 + step, HALO + CZ - 1 - step)
+                live_section(step, first, HALO, to_weighted)
 
     pass_layers(0)
     pass_layers(1)
@@ -428,15 +432,11 @@
         for way in range(2):
             halo(field, way, "received")
     run_sections(lost, lost_scalars, to_recovered)
-    late_live()
-
-    recovered_out = pltpu.make_async_copy(recovered, recovered_ref, local_sem.at[0])
-    recovered_out.start()
 
     third_copies = {}
     for field in range(FIELDS):
         for i, peer in enumerate(peers):
-            copy = pltpu.make_async_remote_copy(
+            third_copies[field, i] = pltpu.make_async_remote_copy(
                 src_ref=weighted.at[peer // 2, peer % 2, field],
                 dst_ref=arrived.at[field, i],
                 send_sem=send3.at[field, i],
@@ -444,8 +444,22 @@
                 device_id={"buddy": peer},
                 device_id_type=MESH,
             )
-            copy.start()
-            third_copies[field, i] = copy
+
+    def send_layers(late):
+        for field in range(FIELDS):
+            for i, peer in enumerate(peers):
+                is_late = jnp.logical_and(crossing, (peer < HALO) == late_below)
+
+                @pl.when(is_late if late else jnp.logical_not(is_late))
+                def _():
+                    third_copies[field, i].start()
+
+    send_layers(False)
+    late_live()
+    send_layers(True)
+
+    recovered_out = pltpu.make_async_copy(recovered, recovered_ref, local_sem.at[0])
+    recovered_out.start()
 
     for field in range(FIELDS):
         total[field, 16] = jnp.zeros((2, CX), jnp.float32)

time: 83.4 us -> 82.2 us (0.986)
  Pallas kernels: 82.5 us -> 81.4 us
    pallas_call x1, Pallas kernels: 80.3 us -> 79.2 us  [body(): pl.pallas_call(kernel, name='recover_and_combine', out_shape=(jax.ShapeDt...]
where the time goes in v4:
time: 82.2 us; the launch traced here: 82.1 us
  Pallas kernels  81.4 us (99%)
    pallas_call x1, Pallas kernels, body(): pl.pallas_call(kernel, name='recover_and_combine', out_shape=(jax.ShapeDt...  79.2 us
    pallas_call x1, Pallas kernels, hand_over(): pl.pallas_call(copies, name='hand_over', out_shape=(jax.ShapeDtypeStruct(...  2.21 us

profile of v4, /device:TPU:7, one launch (start us, length us, event | category | flops | bytes accessed | tf_op | source)
XLA Modules:
  0.0 82.1 jit_solution(18413803663074527563)
XLA Ops:
  0.6 79.2 %recover_and_combine.1 = (f32[5,8,32,256]{3,2,1,0:T(8,128)}, f32[4,5,8,2,256]{4,3,2,1,0:T(2,128)}) custom-call(s32[8,8]{1,0:T(8,128)} %slots_ref.1, s32[1,16]{1,0:T(1,128)} %owners_ref.1, s32[2,1,3]{2,1,0:T(1,128)} %levels_ref.1, f32[1,2]{1,0:T(1,128)} %bitcast.3, f32[8,5,8,4,256]{4,3,2,1,0:T(4,128)} %checkpoint_ref.1, f32[1,5,8,32,256]{4,3,2,1,0:T(8,128)} %live_ref.1), custom_call_target="tpu_custom_call" | custom-call | tf_op jit(solution)/shard_map/recover_and_combine/pallas_call | solution.py:547
  79.8 2.2 %hand_over.1 = (f32[1,5,8,32,256]{4,3,2,1,0:T(8,128)}, f32[4,5,8,2,256]{4,3,2,1,0:T(2,128)}) custom-call(f32[1,5,8,32,256]{4,3,2,1,0:T(8,128)} %bitcast.2, f32[4,5,8,2,256]{4,3,2,1,0:T(2,128)} %get-tuple-element.5.combined_in), custom_call_target="tpu_custom_call" | custom-call | tf_op jit(solution)/shard_map/hand_over/pallas_call | solution.py:524

commit v5 on v4

--- a/solution.py
+++ b/solution.py
@@ -15,7 +15,7 @@
 CX = 256
 HALO = 4
 PEERS = 7
-OFFSETS = ((2, 1), (1, 1), (3, 1), (0, 1), (2, 0), (1, 0), (3, 0))
+OFFSETS = ((0, 1), (2, 1), (1, 1), (3, 1), (2, 0), (1, 0), (3, 0))
 
 
 def stencil(levels_ref, kind):

time: 82.2 us -> 82.3 us (level)
  no operation moved by 1% of the time
where the time goes in v5:
time: 82.3 us; the launch traced here: 82.2 us
  Pallas kernels  81.5 us (99%)
    pallas_call x1, Pallas kernels, body(): pl.pallas_call(kernel, name='recover_and_combine', out_shape=(jax.ShapeDt...  79.3 us
    pallas_call x1, Pallas kernels, hand_over(): pl.pallas_call(copies, name='hand_over', out_shape=(jax.ShapeDtypeStruct(...  2.21 us

profile of v5, /device:TPU:7, one launch (start us, length us, event | category | flops | bytes accessed | tf_op | source)
XLA Modules:
  0.0 82.2 jit_solution(9940879785995956346)
XLA Ops:
  0.6 79.3 %recover_and_combine.1 = (f32[5,8,32,256]{3,2,1,0:T(8,128)}, f32[4,5,8,2,256]{4,3,2,1,0:T(2,128)}) custom-call(s32[8,8]{1,0:T(8,128)} %slots_ref.1, s32[1,16]{1,0:T(1,128)} %owners_ref.1, s32[2,1,3]{2,1,0:T(1,128)} %levels_ref.1, f32[1,2]{1,0:T(1,128)} %bitcast.3, f32[8,5,8,4,256]{4,3,2,1,0:T(4,128)} %checkpoint_ref.1, f32[1,5,8,32,256]{4,3,2,1,0:T(8,128)} %live_ref.1), custom_call_target="tpu_custom_call" | custom-call | tf_op jit(solution)/shard_map/recover_and_combine/pallas_call | solution.py:547
  80.0 2.2 %hand_over.1 = (f32[1,5,8,32,256]{4,3,2,1,0:T(8,128)}, f32[4,5,8,2,256]{4,3,2,1,0:T(2,128)}) custom-call(f32[1,5,8,32,256]{4,3,2,1,0:T(8,128)} %bitcast.2, f32[4,5,8,2,256]{4,3,2,1,0:T(2,128)} %get-tuple-element.5.combined_in), custom_call_target="tpu_custom_call" | custom-call | tf_op jit(solution)/shard_map/hand_over/pallas_call | solution.py:524
